TPU v7x, 32 devices: a whole 2x2x4 slice. The times are simulated.
32 devices in a mesh: groups: 2 (over x), tgt: 16 (over z, y, core).
Axes of the slice: x: 2, y: 2, z: 4, core: 2. Of those that a mesh axis runs over, the one named last changes fastest.
Arguments:
- source_feats: bfloat16 [4096, 1024], P(('groups', 'tgt')), parts along dimension 0, may hold values from -18 to 18
- target_feats: bfloat16 [16384, 1024], P(('groups', 'tgt')), parts along dimension 0, may hold values from -18 to 18
- source_logits: float32 [4096], P('groups'), parts along dimension 0, may hold values from -1.2 to 1.2
- target_logits: float32 [16384], P(('groups', 'tgt')), parts along dimension 0, may hold values from -1 to 3.4
Outputs:
- grad_source: float32 [4096, 1024], P(('groups', 'tgt')), parts along dimension 0
- grad_target: float32 [16384, 1024], P(('groups', 'tgt')), parts along dimension 0
- potential_src: float32 [4096], P('groups'), parts along dimension 0
- potential_tgt: float32 [16384], P(('groups', 'tgt')), parts along dimension 0
There are 2 independent parts, one for each index of `groups`. A program takes and returns all parts, laid end to end along the dimension named above; each array names one. Nothing has to cross between parts.
All inputs are finite; a program needn't handle non-finite values.
Results may differ from a plain program's by a relative error of at most 0.0033.
Values may be sent and summed in bfloat16 or wider, within the bound.
No kernel may reach another device: no remote copies, remote signals or barrier semaphores. Data moves between devices by JAX's collectives and lax.ppermute only.
A program may use at most 64 MiB of HBM per device.

v0:
```python
import math
import jax
import jax.numpy as jnp
from jax import lax
from jax.sharding import PartitionSpec as P

ITERS = 3


def per_device(source_feats, target_feats, source_logits, target_logits):
    width = target_feats.shape[1]
    scale = 1.0 / math.sqrt(width)
    source_count = source_feats.shape[0] * lax.axis_size("tgt")
    target_count = target_feats.shape[0] * lax.axis_size("tgt")
    log_source = source_logits - jnp.log(jnp.sum(jnp.exp(source_logits)))
    target_total = lax.psum(jnp.sum(jnp.exp(target_logits)), "tgt")
    log_target = target_logits - jnp.log(target_total)
    target_sq = jnp.sum(jnp.square(target_feats.astype(jnp.float32)), axis=1)
    gathered = lax.all_gather(source_feats, "tgt", axis=0, tiled=True)
    cross = lax.dot_general(
        gathered, target_feats, (((1,), (1,)), ((), ())), preferred_element_type=jnp.float32
    )
    gathered_sq = jnp.sum(jnp.square(gathered.astype(jnp.float32)), axis=1)
    cost = (gathered_sq[:, None] + target_sq[None, :] - 2.0 * cross) * scale
    potential_tgt = jnp.zeros((target_feats.shape[0],), jnp.float32)
    potential_src = jnp.zeros((source_count,), jnp.float32)
    for step in range(ITERS):
        scores = (log_target + potential_tgt)[None, :] - cost
        top = lax.pmax(jnp.max(scores, axis=1), "tgt")
        total = lax.psum(jnp.sum(jnp.exp(scores - top[:, None]), axis=1), "tgt")
        potential_src = -(top + jnp.log(total))
        column = (log_source + potential_src)[:, None] - cost
        column_top = jnp.max(column, axis=0)
        potential_tgt = -(
            column_top + jnp.log(jnp.sum(jnp.exp(column - column_top[None, :]), axis=0))
        )
    plan = jnp.exp(
        math.log(source_count)
        + (log_source + potential_src)[:, None]
        + (log_target + potential_tgt)[None, :]
        - cost
    ).astype(jnp.bfloat16)
    row_mass = jnp.sum(plan.astype(jnp.float32), axis=1)
    row_part = jnp.dot(plan, target_feats, preferred_element_type=jnp.float32)
    share_part, share_mass = (
        lax.psum_scatter(row_part, "tgt", scatter_dimension=0, tiled=True),
        lax.psum_scatter(row_mass, "tgt", scatter_dimension=0, tiled=True),
    )
    grad_source = share_mass[:, None] * source_feats.astype(jnp.float32) - share_part
    col_part = lax.dot_general(
        plan, gathered, (((0,), (0,)), ((), ())), preferred_element_type=jnp.float32
    )
    col_mass = jnp.sum(plan.astype(jnp.float32), axis=0)
    grad_target = (
        target_count
        / source_count
        * (col_mass[:, None] * target_feats.astype(jnp.float32) - col_part)
    )
    return (grad_source, grad_target, potential_src, potential_tgt)


def solution(mesh):
    return jax.shard_map(
        per_device,
        mesh=mesh,
        in_specs=(
            P(("groups", "tgt"), None),
            P(("groups", "tgt"), None),
            P("groups"),
            P(("groups", "tgt")),
        ),
        out_specs=(
            P(("groups", "tgt"), None),
            P(("groups", "tgt"), None),
            P("groups"),
            P(("groups", "tgt")),
        ),
        check_vma=False,
    )
```

profile of v0, /device:TPU:0, one launch (start us, length us, event | category | flops | bytes accessed | tf_op | source)
XLA Modules:
  0.0 395.1 jit_solution(12551948818565337685)
XLA Ops:
  7.2 0.0 copy-start.5
  7.2 0.0 all-gather.2.cloned.1.call-start
  7.2 0.7 all-gather.2.cloned.1.call-update
  7.9 0.0 reduce-scatter.2.cloned.1.call-start
  8.0 1.3 exponential_reduce_fusion.7
  9.3 36.0 %psum.28 = f32[]{:T(128)} all-reduce(f32[]{:T(128)} %exponential_reduce_fusion.7), channel_id=1, replica_groups=mesh['groups'=2,'tgt'=16] {'tgt'}, use_global_device_ids=true, to_apply=%region_2.0 | all-reduce | flops 1 | bytes 8 | tf_op jit(solution)/shard_map/psum | solution.py:16
  45.9 1.3 exponential_reduce_fusion.6
  47.9 1.5 fusion
  49.5 0.7 broadcast_subtract_fusion
  50.2 13.4 %all-gather.2.cloned.1.call-done = bf16[2048,1024]{1,0:T(8,128)(2,1)} async-done(((bf16[128,1024]{1,0:T(8,128)(2,1)}), bf16[2048,1024]{1,0:T(8,128)(2,1)}) %all-gather.2.cloned.1.call-update) | async-done | bytes 4194320 | tf_op jit(solution)/shard_map/all_gather | solution.py:19
  63.6 0.0 copy-start.3
  63.6 3.2 multiply_reduce_fusion
  66.8 0.0 copy-done.5
  66.8 0.2 copy-done.3
  67.0 4.8 %subtract_reduce_fusion.5 = (f32[2048]{0:T(1024)S(1)}, f32[2048,512]{1,0:T(8,128)}) fusion(f32[512]{0:T(512)S(1)} %broadcast_subtract_fusion, bf16[2048,1024]{1,0:T(8,128)(2,1)S(1)} %copy-done.3, bf16[512,1024]{1,0:T(8,128)(2,1)S(1)} %copy-done.5, f32[512]{0:T(512)S(1)} %fusion, f32[2048]{0:T(1024)S(1)} %multiply_reduce_fusion), kind=kOutput, calls=%fused_computation.16 | convolution fusion | flops 2153773056 | bytes 9457664 | tf_op jit(solution)/shard_map/dot_general | solution.py:20
  71.8 0.0 copy-start.6
  71.8 31.6 %pmax.21 = f32[2048]{0:T(1024)S(1)} all-reduce(f32[2048]{0:T(1024)S(1)} %get-tuple-element.12), channel_id=1, replica_groups=mesh['groups'=2,'tgt'=16] {'tgt'}, use_global_device_ids=true, to_apply=%region_6.0 | all-reduce | flops 2048 | bytes 16384 | tf_op jit(solution)/shard_map/pmax | solution.py:29
  103.5 3.2 exponential_reduce_fusion.5
  106.7 30.0 %psum.29 = f32[2048]{0:T(1024)S(1)} all-reduce(f32[2048]{0:T(1024)S(1)} %exponential_reduce_fusion.5), channel_id=1, replica_groups=mesh['groups'=2,'tgt'=16] {'tgt'}, use_global_device_ids=true, to_apply=%region_8.0 | all-reduce | flops 2048 | bytes 16384 | tf_op jit(solution)/shard_map/psum | solution.py:30
  136.7 0.0 copy-done.6
  136.7 0.0 copy-start
  136.7 0.0 copy-start.7
  136.8 2.7 subtract_reduce_fusion.4
  139.4 0.7 copy-done
  140.2 0.8 exponential_reduce_fusion.4
  140.9 0.0 copy-done.7
  141.0 0.4 subtract_reduce_fusion.3
  141.3 30.0 %pmax.22 = f32[2048]{0:T(1024)S(1)} all-reduce(f32[2048]{0:T(1024)S(1)} %subtract_reduce_fusion.3), channel_id=1, replica_groups=mesh['groups'=2,'tgt'=16] {'tgt'}, use_global_device_ids=true, to_apply=%region_12.0 | all-reduce | flops 2048 | bytes 16384 | tf_op jit(solution)/shard_map/pmax | solution.py:29
  171.3 3.2 exponential_reduce_fusion.3
  174.5 30.0 %psum.30 = f32[2048]{0:T(1024)S(1)} all-reduce(f32[2048]{0:T(1024)S(1)} %exponential_reduce_fusion.3), channel_id=1, replica_groups=mesh['groups'=2,'tgt'=16] {'tgt'}, use_global_device_ids=true, to_apply=%region_14.0 | all-reduce | flops 2048 | bytes 16384 | tf_op jit(solution)/shard_map/psum | solution.py:30
  204.5 0.0 copy-start.1
  204.6 2.7 subtract_reduce_fusion.2
  207.3 0.7 copy-done.1
  208.0 0.8 exponential_reduce_fusion.2
  208.8 0.4 subtract_reduce_fusion.1
  209.1 30.0 %pmax.23 = f32[2048]{0:T(1024)S(1)} all-reduce(f32[2048]{0:T(1024)S(1)} %subtract_reduce_fusion.1), channel_id=1, replica_groups=mesh['groups'=2,'tgt'=16] {'tgt'}, use_global_device_ids=true, to_apply=%region_18.0 | all-reduce | flops 2048 | bytes 16384 | tf_op jit(solution)/shard_map/pmax | solution.py:29
  239.1 3.2 exponential_reduce_fusion.1
  242.3 30.2 %psum.31 = f32[2048]{0:T(1024)S(1)} all-reduce(f32[2048]{0:T(1024)S(1)} %exponential_reduce_fusion.1), channel_id=1, replica_groups=mesh['groups'=2,'tgt'=16] {'tgt'}, use_global_device_ids=true, to_apply=%region_20.0 | all-reduce | flops 2048 | bytes 16384 | tf_op jit(solution)/shard_map/psum | solution.py:30
  272.5 0.0 copy-start.2
  272.5 0.6 broadcast_add_fusion
  273.1 2.9 subtract_reduce_fusion
  276.0 0.0 copy-done.2
  276.0 0.8 exponential_reduce_fusion
  276.8 0.6 fusion.3
  277.4 1.3 convert_reduce_fusion
  278.7 5.6 %fusion.4 = f32[2048,1024]{1,0:T(8,128)} fusion(bf16[2048,512]{1,0:T(8,128)(2,1)S(1)} %get-tuple-element.6, bf16[512,1024]{1,0:T(8,128)(2,1)S(1)} %copy-done.5), kind=kOutput, calls=%fused_computation.35 | convolution fusion | flops 2147483648 | bytes 11534336 | tf_op jit(solution)/shard_map/dot_general | solution.py:44
  284.3 0.0 copy-start.8
  284.3 0.0 reduce-scatter.2.cloned.1.call-update
  284.3 0.6 copy-done.8
  284.9 0.6 dynamic-slice
  286.2 30.1 %all-reduce = f32[2048]{0:T(1024)S(1)} all-reduce(f32[2048]{0:T(1024)S(1)} %get-tuple-element.5), channel_id=2, replica_groups=mesh['groups'=2,'tgt'=16] {'tgt'}, use_global_device_ids=true, to_apply=%region_24.0.clone | all-reduce | flops 2048 | bytes 16384
  316.3 0.1 dynamic-slice.1
  316.3 0.0 copy-start.4
  316.3 5.9 %fusion.2 = f32[512,1024]{1,0:T(8,128)} fusion(bf16[512,1024]{1,0:T(8,128)(2,1)S(1)} %copy-done.5, bf16[2048,512]{1,0:T(8,128)(2,1)S(1)} %get-tuple-element.6, bf16[2048,1024]{1,0:T(8,128)(2,1)} %all-gather.2.cloned.1.call-done, f32[512]{0:T(512)S(1)} %get-tuple-element.4), kind=kOutput, calls=%fused_computation.21 | convolution fusion | flops 2149580800 | bytes 9439232 | tf_op jit(solution)/shard_map/dot_general | solution.py:50
  322.2 64.0 %reduce-scatter.2.cloned.1.call-done = f32[128,1024]{1,0:T(8,128)} async-done(((f32[2048,1024]{1,0:T(8,128)}), f32[128,1024]{1,0:T(8,128)}) %reduce-scatter.2.cloned.1.call-update) | async-done | bytes 524304 | tf_op jit(solution)/shard_map/reduce_scatter | solution.py:46
  386.3 0.0 copy-done.4
  386.3 2.0 multiply_subtract_fusion
  (4 shorter events, 0.0 us)
Async XLA Ops:
  7.2 59.6 %copy-start.5 = (bf16[512,1024]{1,0:T(8,128)(2,1)S(1)}, bf16[512,1024]{1,0:T(8,128)(2,1)}, u32[]{:S(2)}) copy-start(bf16[512,1024]{1,0:T(8,128)(2,1)} %param.5) | copy-start | bytes 3145732
  7.2 56.4 %all-gather.2.cloned.1.call-start = ((), (), s32[]{:S(2)}) async-start(), calls=%async_computation.1 | async-start | bytes 4456448 | tf_op jit(solution)/shard_map/all_gather | solution.py:19
  7.9 378.4 %reduce-scatter.2.cloned.1.call-start = ((), (), s32[]{:S(2)}) async-start(), calls=%async_computation.2 | async-start | bytes 8912896 | tf_op jit(solution)/shard_map/reduce_scatter | solution.py:46
  63.6 3.4 copy-start.3
  71.8 64.9 %copy-start.6 = (f32[2048]{0:T(1024)S(1)}, f32[2048]{0:T(1024)}, u32[]{:S(2)}) copy-start(f32[2048]{0:T(1024)} %param.6) | copy-start | bytes 24580
  136.7 3.5 copy-start
  136.7 4.2 %copy-start.7 = (f32[512]{0:T(512)S(1)}, f32[512]{0:T(512)}, u32[]{:S(2)}) copy-start(f32[512]{0:T(512)} %param.7) | copy-start | bytes 6148
  204.5 3.5 copy-start.1
  272.5 3.5 copy-start.2
  284.3 0.7 copy-start.8
  316.3 69.9 %copy-start.4 = (bf16[128,1024]{1,0:T(8,128)(2,1)S(1)}, bf16[128,1024]{1,0:T(8,128)(2,1)}, u32[]{:S(2)}) copy-start(bf16[128,1024]{1,0:T(8,128)(2,1)} %param.4) | copy-start | bytes 786436
Sparse Core Ops, SparseCore 0:
  10.2 53.3 all-gather.1
  284.4 101.8 reduce-scatter.1
where the time goes:
time: 396 us; the launch traced here: 395 us
  blocking collectives  248 us (63%)
  waiting for transfers between devices  78.1 us (20%)
  other arithmetic  33.4 us (8%)
  matrix products  16.3 us (4%)
  between operations  16.3 us (4%)
    pmax x3, blocking collectives, per_device(): top = lax.pmax(jnp.max(scores, axis=1), 'tgt')  91.6 us
    psum x3, blocking collectives, per_device(): total = lax.psum(jnp.sum(jnp.exp(scores - top[:, None]), axis=1), 'tgt')  90.2 us
    reduce_scatter x1, waiting for transfers between devices, per_device(): lax.psum_scatter(row_part, 'tgt', scatter_dimension=0, tiled=True)  64 us
    psum x1, blocking collectives, per_device(): target_total = lax.psum(jnp.sum(jnp.exp(target_logits)), 'tgt')  36 us
    unnamed x1, blocking collectives  30.1 us
    all_gather x1, waiting for transfers between devices, per_device(): gathered = lax.all_gather(source_feats, 'tgt', axis=0, tiled=True)  13.4 us
    reduce_sum x3, other arithmetic, per_device(): total = lax.psum(jnp.sum(jnp.exp(scores - top[:, None]), axis=1), 'tgt')  9.62 us
    reduce_max x3, other arithmetic, per_device(): column_top = jnp.max(column, axis=0)  8.23 us
  transfers between devices with their start and end apart: 2, of which 2 were waited for; matrix products, arithmetic and copies ran while one was open for 3% of the time, Pallas kernels for 0%

commit v1 on v0

--- a/solution.py
+++ b/solution.py
@@ -5,6 +5,11 @@
 from jax.sharding import PartitionSpec as P
 
 ITERS = 3
+
+
+def zone_compute(q_in):
+    arr_now = lax.all_gather(q_in, axis_name="tgt")
+    return jnp.sum(arr_now, axis=0)
 
 
 def per_device(source_feats, target_feats, source_logits, target_logits):
@@ -27,7 +32,7 @@
     for step in range(ITERS):
         scores = (log_target + potential_tgt)[None, :] - cost
         top = lax.pmax(jnp.max(scores, axis=1), "tgt")
-        total = lax.psum(jnp.sum(jnp.exp(scores - top[:, None]), axis=1), "tgt")
+        total = zone_compute(jnp.sum(jnp.exp(scores - top[:, None]), axis=1))
         potential_src = -(top + jnp.log(total))
         column = (log_source + potential_src)[:, None] - cost
         column_top = jnp.max(column, axis=0)

time: 396 us -> 364 us (0.919)
  blocking collectives: 248 us -> 216 us
    psum x3 -> x0, blocking collectives: 90.2 us -> none  [per_device(): total = lax.psum(jnp.sum(jnp.exp(scores - top[:, None]), axis=1), 'tgt')]
    all_gather x0 -> x3, blocking collectives: none -> 52.7 us  [zone_compute(): arr_now = lax.all_gather(q_in, axis_name='tgt')]
    reduce_sum x3 -> x6, other arithmetic: 9.62 us -> 9.68 us  [the longest x3 9.6 us: per_device(): total = zone_compute(jnp.sum(jnp.exp(scores - top[:, None]), axis=1))]
where the time goes in v1:
time: 364 us; the launch traced here: 363 us
  blocking collectives  216 us (59%)
  waiting for transfers between devices  77.6 us (21%)
  other arithmetic  33.5 us (9%)
  matrix products  16.3 us (4%)
  between operations  16.3 us (4%)
    pmax x3, blocking collectives, per_device(): top = lax.pmax(jnp.max(scores, axis=1), 'tgt')  95.5 us
    reduce_scatter x1, waiting for transfers between devices, per_device(): lax.psum_scatter(row_part, 'tgt', scatter_dimension=0, tiled=True)  63.5 us
    all_gather x3, blocking collectives, zone_compute(): arr_now = lax.all_gather(q_in, axis_name='tgt')  52.7 us
    psum x1, blocking collectives, per_device(): target_total = lax.psum(jnp.sum(jnp.exp(target_logits)), 'tgt')  36 us
    unnamed x1, blocking collectives  32 us
    all_gather x1, waiting for transfers between devices, per_device(): gathered = lax.all_gather(source_feats, 'tgt', axis=0, tiled=True)  13.4 us
    reduce_sum x3, other arithmetic, per_device(): total = zone_compute(jnp.sum(jnp.exp(scores - top[:, None]), axis=1))  9.6 us
    reduce_max x3, other arithmetic, per_device(): column_top = jnp.max(column, axis=0)  8.23 us
  transfers between devices with their start and end apart: 2, of which 2 were waited for; matrix products, arithmetic and copies ran while one was open for 3% of the time, Pallas kernels for 0%

profile of v1, /device:TPU:0, one launch (start us, length us, event | category | flops | bytes accessed | tf_op | source)
XLA Modules:
  0.0 363.1 jit_solution(6604175976844115843)
XLA Ops:
  7.2 0.0 copy-start.5
  7.2 0.0 all-gather.5.cloned.1.call-start
  7.2 0.7 all-gather.5.cloned.1.call-update
  7.9 0.0 reduce-scatter.2.cloned.1.call-start
  8.0 1.3 exponential_reduce_fusion.7
  9.3 36.0 %psum.7 = f32[]{:T(128)} all-reduce(f32[]{:T(128)} %exponential_reduce_fusion.7), channel_id=1, replica_groups=mesh['groups'=2,'tgt'=16] {'tgt'}, use_global_device_ids=true, to_apply=%region_2.0 | all-reduce | flops 1 | bytes 8 | tf_op jit(solution)/shard_map/psum | solution.py:21
  45.9 1.3 exponential_reduce_fusion.6
  47.9 1.5 fusion
  49.5 0.7 broadcast_subtract_fusion
  50.2 13.4 %all-gather.5.cloned.1.call-done = bf16[2048,1024]{1,0:T(8,128)(2,1)} async-done(((bf16[128,1024]{1,0:T(8,128)(2,1)}), bf16[2048,1024]{1,0:T(8,128)(2,1)}) %all-gather.5.cloned.1.call-update) | async-done | bytes 4194320 | tf_op jit(solution)/shard_map/all_gather | solution.py:24
  63.6 0.0 copy-start.3
  63.6 3.2 multiply_reduce_fusion
  66.8 0.0 copy-done.5
  66.8 0.2 copy-done.3
  67.0 4.8 %subtract_reduce_fusion.5 = (f32[2048]{0:T(1024)S(1)}, f32[2048,512]{1,0:T(8,128)}) fusion(f32[512]{0:T(512)S(1)} %broadcast_subtract_fusion, bf16[2048,1024]{1,0:T(8,128)(2,1)S(1)} %copy-done.3, bf16[512,1024]{1,0:T(8,128)(2,1)S(1)} %copy-done.5, f32[512]{0:T(512)S(1)} %fusion, f32[2048]{0:T(1024)S(1)} %multiply_reduce_fusion), kind=kOutput, calls=%fused_computation.16 | convolution fusion | flops 2153773056 | bytes 9457664 | tf_op jit(solution)/shard_map/dot_general | solution.py:25
  71.8 0.0 copy-start.6
  71.8 31.6 %pmax.21 = f32[2048]{0:T(1024)S(1)} all-reduce(f32[2048]{0:T(1024)S(1)} %get-tuple-element.12), channel_id=1, replica_groups=mesh['groups'=2,'tgt'=16] {'tgt'}, use_global_device_ids=true, to_apply=%region_6.0 | all-reduce | flops 2048 | bytes 16384 | tf_op jit(solution)/shard_map/pmax | solution.py:34
  103.5 3.2 exponential_reduce_fusion.5
  106.7 17.5 %all-gather = f32[32768]{0:T(1024)S(1)} all-gather(f32[2048]{0:T(1024)S(1)} %exponential_reduce_fusion.5), channel_id=2, replica_groups=mesh['groups'=2,'tgt'=16] {'tgt'}, dimensions={0}, use_global_device_ids=true | all-gather | bytes 139264 | tf_op jit(solution)/shard_map/all_gather | solution.py:11
  124.2 0.0 copy-done.6
  124.3 0.0 copy-start
  124.3 0.0 copy-start.7
  124.3 2.7 subtract_reduce_fusion.4
  127.0 0.7 copy-done
  127.7 0.8 exponential_reduce_fusion.4
  128.5 0.0 copy-done.7
  128.5 0.4 subtract_reduce_fusion.3
  128.9 31.9 %pmax.22 = f32[2048]{0:T(1024)S(1)} all-reduce(f32[2048]{0:T(1024)S(1)} %subtract_reduce_fusion.3), channel_id=1, replica_groups=mesh['groups'=2,'tgt'=16] {'tgt'}, use_global_device_ids=true, to_apply=%region_12.0 | all-reduce | flops 2048 | bytes 16384 | tf_op jit(solution)/shard_map/pmax | solution.py:34
  160.8 3.2 exponential_reduce_fusion.3
  164.0 17.5 %all-gather.1 = f32[32768]{0:T(1024)S(1)} all-gather(f32[2048]{0:T(1024)S(1)} %exponential_reduce_fusion.3), channel_id=3, replica_groups=mesh['groups'=2,'tgt'=16] {'tgt'}, dimensions={0}, use_global_device_ids=true | all-gather | bytes 139264 | tf_op jit(solution)/shard_map/all_gather | solution.py:11
  181.6 0.0 copy-start.1
  181.6 2.7 subtract_reduce_fusion.2
  184.3 0.7 copy-done.1
  185.0 0.8 exponential_reduce_fusion.2
  185.8 0.4 subtract_reduce_fusion.1
  186.2 31.9 %pmax.23 = f32[2048]{0:T(1024)S(1)} all-reduce(f32[2048]{0:T(1024)S(1)} %subtract_reduce_fusion.1), channel_id=1, replica_groups=mesh['groups'=2,'tgt'=16] {'tgt'}, use_global_device_ids=true, to_apply=%region_18.0 | all-reduce | flops 2048 | bytes 16384 | tf_op jit(solution)/shard_map/pmax | solution.py:34
  218.1 3.2 exponential_reduce_fusion.1
  221.3 17.7 %all-gather.2 = f32[32768]{0:T(1024)S(1)} all-gather(f32[2048]{0:T(1024)S(1)} %exponential_reduce_fusion.1), channel_id=4, replica_groups=mesh['groups'=2,'tgt'=16] {'tgt'}, dimensions={0}, use_global_device_ids=true | all-gather | bytes 139264 | tf_op jit(solution)/shard_map/all_gather | solution.py:11
  239.1 0.0 copy-start.2
  239.1 0.6 broadcast_add_fusion
  239.7 2.8 subtract_reduce_fusion
  242.6 0.0 copy-done.2
  242.6 0.8 exponential_reduce_fusion
  243.3 0.6 fusion.3
  243.9 1.3 convert_reduce_fusion
  245.3 5.6 %fusion.4 = f32[2048,1024]{1,0:T(8,128)} fusion(bf16[2048,512]{1,0:T(8,128)(2,1)S(1)} %get-tuple-element.6, bf16[512,1024]{1,0:T(8,128)(2,1)S(1)} %copy-done.5), kind=kOutput, calls=%fused_computation.35 | convolution fusion | flops 2147483648 | bytes 11534336 | tf_op jit(solution)/shard_map/dot_general | solution.py:49
  250.8 0.0 copy-start.8
  250.8 0.0 reduce-scatter.2.cloned.1.call-update
  250.9 0.6 copy-done.8
  251.5 0.6 dynamic-slice
  252.7 32.0 %all-reduce = f32[2048]{0:T(1024)S(1)} all-reduce(f32[2048]{0:T(1024)S(1)} %get-tuple-element.5), channel_id=5, replica_groups=mesh['groups'=2,'tgt'=16] {'tgt'}, use_global_device_ids=true, to_apply=%region_24.0.clone | all-reduce | flops 2048 | bytes 16384
  284.8 0.1 dynamic-slice.1
  284.8 0.0 copy-start.4
  284.8 5.9 %fusion.2 = f32[512,1024]{1,0:T(8,128)} fusion(bf16[512,1024]{1,0:T(8,128)(2,1)S(1)} %copy-done.5, bf16[2048,512]{1,0:T(8,128)(2,1)S(1)} %get-tuple-element.6, bf16[2048,1024]{1,0:T(8,128)(2,1)} %all-gather.5.cloned.1.call-done, f32[512]{0:T(512)S(1)} %get-tuple-element.4), kind=kOutput, calls=%fused_computation.21 | convolution fusion | flops 2149580800 | bytes 9439232 | tf_op jit(solution)/shard_map/dot_general | solution.py:55
  290.7 63.5 %reduce-scatter.2.cloned.1.call-done = f32[128,1024]{1,0:T(8,128)} async-done(((f32[2048,1024]{1,0:T(8,128)}), f32[128,1024]{1,0:T(8,128)}) %reduce-scatter.2.cloned.1.call-update) | async-done | bytes 524304 | tf_op jit(solution)/shard_map/reduce_scatter | solution.py:51
  354.3 0.0 copy-done.4
  354.3 2.0 multiply_subtract_fusion
  (10 shorter events, 0.2 us)
Async XLA Ops:
  7.2 59.6 %copy-start.5 = (bf16[512,1024]{1,0:T(8,128)(2,1)S(1)}, bf16[512,1024]{1,0:T(8,128)(2,1)}, u32[]{:S(2)}) copy-start(bf16[512,1024]{1,0:T(8,128)(2,1)} %param.5) | copy-start | bytes 3145732
  7.2 56.4 %all-gather.5.cloned.1.call-start = ((), (), s32[]{:S(2)}) async-start(), calls=%async_computation.1 | async-start | bytes 4456448 | tf_op jit(solution)/shard_map/all_gather | solution.py:24
  7.9 346.4 %reduce-scatter.2.cloned.1.call-start = ((), (), s32[]{:S(2)}) async-start(), calls=%async_computation.2 | async-start | bytes 8912896 | tf_op jit(solution)/shard_map/reduce_scatter | solution.py:51
  63.6 3.4 copy-start.3
  71.8 52.4 %copy-start.6 = (f32[2048]{0:T(1024)S(1)}, f32[2048]{0:T(1024)}, u32[]{:S(2)}) copy-start(f32[2048]{0:T(1024)} %param.6) | copy-start | bytes 24580
  124.3 3.5 copy-start
  124.3 4.2 %copy-start.7 = (f32[512]{0:T(512)S(1)}, f32[512]{0:T(512)}, u32[]{:S(2)}) copy-start(f32[512]{0:T(512)} %param.7) | copy-start | bytes 6148
  181.6 3.5 copy-start.1
  239.1 3.5 copy-start.2
  250.8 0.7 copy-start.8
  284.8 69.4 %copy-start.4 = (bf16[128,1024]{1,0:T(8,128)(2,1)S(1)}, bf16[128,1024]{1,0:T(8,128)(2,1)}, u32[]{:S(2)}) copy-start(bf16[128,1024]{1,0:T(8,128)(2,1)} %param.4) | copy-start | bytes 786436
Sparse Core Ops, SparseCore 0:
  10.2 53.3 all-gather.4
  251.0 103.2 reduce-scatter.1
